TPU v7x, 512 devices: a whole 4x8x8 slice. The times are simulated.
512 devices in a mesh: space: 128 (over x, y, z_hi, core), modes: 4 (over z_lo).
Axes of the slice: x: 4, y: 8, z: 8 (z_hi: 2, z_lo: 4; z = z_hi * 4 + z_lo), core: 2. Of those that a mesh axis runs over, the one named last changes fastest.
Arguments:
- voltage_expansion: float32 [220, 128, 2048], P('modes', 'space'), may hold values from -6 to 6
- current_injection: float32 [220, 128, 2048], P('modes', 'space'), may hold values from -48 to 48
- thermal_state: float32 [220, 128, 2048], P('modes', 'space'), may hold values from -6 to 6
- average_electric_transport: float32 [128, 2048], P('space'), may hold values from 0.5 to 4
- material_zone: int32 [128, 2048], P('space'), may hold values from 0 to 3
- zone_relative_response: float32 [4, 9], replicated, may hold values from 0.02 to 0.12
- polynomial_exponent_rows: int32 [220, 9], replicated, may hold values from 0 to 3, as said below
- quadrature_abscissa_choice: int32 [512, 9], replicated, may hold values from 0 to 4
- quadrature_integer_share: int32 [512], replicated, may hold values from 1 to 1024
Outputs:
- relaxed_voltage: float32 [220, 128, 2048], P('modes', 'space')
- advanced_thermal_state: float32 [220, 128, 2048], P('modes', 'space')
Inputs may be any that keep to these rules, and one draw needn't show every extreme that they name: `polynomial_exponent_rows`: the rows are the 220 multi-indices of total degree at most 3 over 9 parameters, each once.
All inputs are finite; a program needn't handle non-finite values.
Results may differ from a plain program's by a relative error of at most 0.0003.
Values sent between devices are 32-bit elements; how exact they have to be, the bound alone decides.
A program may use at most 64 MiB of HBM per device.

v0:
```python
import jax
import jax.numpy as jnp
from jax import lax
from jax.sharding import PartitionSpec as P

NY = 256
NZ = 8
HERMITE_NODES = (
    0.0,
    1.355626179974266,
    -1.355626179974266,
    2.8569700138728056,
    -2.8569700138728056,
)


def padded_2(block, sides, width):
    for axis, dim in sides:
        count = lax.axis_size(axis)
        forward = [(i, i + 1) for i in range(count - 1)]
        backward = [(target, source) for source, target in forward]
        low = lax.ppermute(
            lax.slice_in_dim(block, block.shape[dim] - width, None, axis=dim), axis, forward
        )
        high = lax.ppermute(lax.slice_in_dim(block, 0, width, axis=dim), axis, backward)
        block = jnp.concatenate([low, block, high], axis=dim)
    return block


def neighbours(field):
    column_ids = jnp.arange(field.shape[-1])
    depth_pos = column_ids % NZ
    row_pos = column_ids // NZ
    z_next = jnp.where(depth_pos < NZ - 1, jnp.roll(field, -1, -1), 0.0)
    z_prev = jnp.where(depth_pos > 0, jnp.roll(field, 1, -1), 0.0)
    y_next = jnp.where(row_pos < NY - 1, jnp.roll(field, -NZ, -1), 0.0)
    y_prev = jnp.where(row_pos > 0, jnp.roll(field, NZ, -1), 0.0)
    return (z_next, z_prev, y_next, y_prev)


def diffusion_operator_weights(padded):
    center = padded[..., 1:-1, :]
    z_next, z_prev, y_next, y_prev = neighbours(center)
    return (
        6.0 * center - padded[..., 2:, :] - padded[..., :-2, :] - z_next - z_prev - y_next - y_prev
    )


def gradient(padded):
    center = padded[..., 1:-1, :]
    z_next, z_prev, y_next, y_prev = neighbours(center)
    along_x = (padded[..., 2:, :] - padded[..., :-2, :]) * 0.5
    along_y = (y_next - y_prev) * 0.5
    along_z = (z_next - z_prev) * 0.5
    return jnp.stack([along_x, along_y, along_z])


def coupling(row_table, col_table):
    offsets = row_table[:, None, :] - col_table[None, :, :]
    differ_count = jnp.sum((offsets != 0).astype(jnp.int32), axis=2)
    layers = [jnp.where(differ_count == 0, 1.0, 0.0).astype(jnp.float32)]
    for which_param in range(row_table.shape[1]):
        larger = jnp.maximum(
            row_table[:, None, which_param], col_table[None, :, which_param]
        ).astype(jnp.float32)
        linked = (jnp.abs(offsets[:, :, which_param]) == 1) & (differ_count == 1)
        layers.append(jnp.where(linked, jnp.sqrt(larger), 0.0))
    return jnp.stack(layers)


def node_values(quadrature_abscissa_choice):
    node_vals = jnp.zeros(quadrature_abscissa_choice.shape, jnp.float32)
    for which_node in range(5):
        node_vals = node_vals + jnp.where(
            quadrature_abscissa_choice == which_node, HERMITE_NODES[which_node], 0.0
        )
    return node_vals


def basis_values(polynomial_exponent_rows, node_vals):
    poly_terms = [
        jnp.ones_like(node_vals),
        node_vals,
        (node_vals * node_vals - 1.0) / jnp.sqrt(2.0),
        (node_vals * node_vals * node_vals - 3.0 * node_vals) / jnp.sqrt(6.0),
    ]
    basis_vals = jnp.ones((node_vals.shape[0], polynomial_exponent_rows.shape[0]), jnp.float32)
    for which_param in range(polynomial_exponent_rows.shape[1]):
        degree = polynomial_exponent_rows[:, which_param]
        factor = jnp.zeros_like(basis_vals)
        for which_deg in range(4):
            factor = factor + jnp.where(
                degree[None, :] == which_deg, poly_terms[which_deg][:, which_param][:, None], 0.0
            )
        basis_vals = basis_vals * factor
    return basis_vals


def on_device(
    voltage_expansion,
    current_injection,
    thermal_state,
    average_electric_transport,
    material_zone,
    zone_relative_response,
    polynomial_exponent_rows,
    quadrature_abscissa_choice,
    quadrature_integer_share,
):
    hp = lax.Precision.HIGHEST
    modes_here = voltage_expansion.shape[0]
    planes = voltage_expansion.shape[1]
    columns = voltage_expansion.shape[2]
    cell_count = planes * columns
    nreg = zone_relative_response.shape[0]
    all_modes = polynomial_exponent_rows.shape[0]
    num_points = quadrature_integer_share.shape[0]
    first_mode = lax.axis_index("modes") * modes_here
    own_table = lax.dynamic_slice_in_dim(polynomial_exponent_rows, first_mode, modes_here, 0)
    bordered_quantities = padded_2(
        jnp.stack([voltage_expansion, thermal_state]), (("space", 2),), 1
    )
    pot_padded = bordered_quantities[0]
    thermal_state_bordered = bordered_quantities[1]
    sens_cell = jnp.zeros((zone_relative_response.shape[1],) + material_zone.shape, jnp.float32)
    for which_region in range(nreg):
        sens_cell = sens_cell + jnp.where(
            material_zone[None] == which_region,
            zone_relative_response[which_region][:, None, None],
            0.0,
        )
    coeff = (
        jnp.concatenate([jnp.ones((1,) + material_zone.shape, jnp.float32), sens_cell])
        * average_electric_transport
    )
    coeff_flat = coeff.reshape(coeff.shape[0], cell_count)
    flat_rough = diffusion_operator_weights(pot_padded).reshape(modes_here, cell_count)
    row_coup = coupling(own_table, polynomial_exponent_rows)
    mixed = jnp.einsum(
        "mij,jc->mic",
        row_coup,
        lax.all_gather(flat_rough, "modes", axis=0, tiled=True),
        precision=hp,
    )
    applied = jnp.sum(coeff_flat[:, None, :] * mixed, axis=0)
    applied = applied.reshape(modes_here, planes, columns)
    relaxed_voltage = voltage_expansion + 0.8 * (current_injection - applied) / (
        6.0 * average_electric_transport
    )
    node_vals = node_values(quadrature_abscissa_choice)
    basis_vals = basis_values(polynomial_exponent_rows, node_vals)
    new_padded = padded_2(relaxed_voltage, (("space", 1),), 1)
    grads = gradient(new_padded)
    point_grads = jnp.einsum(
        "qi,kixn->kqxn",
        basis_vals,
        lax.all_to_all(grads, "modes", split_axis=3, concat_axis=1, tiled=True),
        precision=hp,
    )
    quarter = columns // lax.axis_size("modes")
    offset = lax.axis_index("modes") * quarter
    cond_part = lax.dynamic_slice_in_dim(average_electric_transport, offset, quarter, 1)
    region_part = lax.dynamic_slice_in_dim(material_zone, offset, quarter, 1)
    cond_lift = 1.0 + jnp.dot(zone_relative_response, node_vals.T, precision=hp)
    spread = jnp.zeros((num_points, planes, quarter), jnp.float32)
    for which_region in range(nreg):
        spread = spread + jnp.where(
            region_part[None] == which_region, cond_lift[which_region][:, None, None], 0.0
        )
    joule_heat = cond_part * spread * jnp.sum(point_grads * point_grads, axis=0)
    weighted = (
        basis_vals.T
        * quadrature_integer_share[None, :].astype(jnp.float32)
        / (512.0 * num_points * all_modes)
    )
    heat_points = jnp.einsum("iq,qxn->ixn", weighted, joule_heat, precision=hp)
    thermal_expansion_terms = lax.all_to_all(
        heat_points, "modes", split_axis=0, concat_axis=2, tiled=True
    )
    advanced_thermal_state = thermal_state + 0.1 * (
        thermal_expansion_terms - 1.5 * diffusion_operator_weights(thermal_state_bordered)
    )
    return (relaxed_voltage, advanced_thermal_state)


def solution(mesh):
    in_specs = (
        P("modes", "space", None),
        P("modes", "space", None),
        P("modes", "space", None),
        P("space", None),
        P("space", None),
        P(),
        P(),
        P(),
        P(),
    )
    out_specs = (P("modes", "space", None), P("modes", "space", None))
    return jax.shard_map(
        on_device, mesh=mesh, in_specs=in_specs, out_specs=out_specs, check_vma=False
    )
```

profile of v0, /device:TPU:59, one launch (start us, length us, event | category | flops | bytes accessed | tf_op | source)
XLA Modules:
  0.0 265.5 jit_solution(5457627602112726379)
XLA Ops:
  7.2 1.4 copy_bitcast_fusion
  8.8 0.7 copy.62
  9.5 2.6 collective-permute-start.1
  12.1 10.5 %collective-permute-start = (f32[2,55,1,2048]{3,0,2,1:T(2,128)S(1)}, f32[2,55,1,2048]{3,0,2,1:T(2,128)}, u32[]{:S(2)}, u32[]{:S(2)}) collective-permute-start(f32[2,55,1,2048]{3,0,2,1:T(2,128)S(1)} %copy.62), channel_id=1, source_target_pairs={{0,4},{4,8},{8,12},{12,16},{16,20},{20,24},{24,28},{28,32},{32,36}... | collective-permute-start | bytes 2703368 | tf_op jit(solution)/shard_map/ppermute | solution.py:22
  22.9 0.1 broadcast_subtract_fusion
  23.0 0.6 bitcast_dynamic-update-slice_fusion
  23.8 0.6 compare_reduce_fusion.7
  24.5 0.7 select_dynamic-update-slice_fusion.8
  25.2 0.7 select_dynamic-update-slice_fusion.7
  25.9 0.7 select_dynamic-update-slice_fusion.6
  26.7 0.7 select_dynamic-update-slice_fusion.5
  27.4 27.7 %collective-permute-done.1 = f32[2,55,1,2048]{3,0,2,1:T(2,128)} collective-permute-done((f32[2,55,1,2048]{3,0,2,1:T(2,128)S(1)}, f32[2,55,1,2048]{3,0,2,1:T(2,128)}, u32[]{:S(2)}, u32[]{:S(2)}) %collective-permute-start.1) | collective-permute-done | bytes 901152 | tf_op jit(solution)/shard_map/ppermute | solution.py:25
  55.0 1.7 copy.65
  56.7 8.6 %collective-permute-done = f32[2,55,1,2048]{3,0,2,1:T(2,128)} collective-permute-done((f32[2,55,1,2048]{3,0,2,1:T(2,128)S(1)}, f32[2,55,1,2048]{3,0,2,1:T(2,128)}, u32[]{:S(2)}, u32[]{:S(2)}) %collective-permute-start) | collective-permute-done | bytes 901152 | tf_op jit(solution)/shard_map/ppermute | solution.py:22
  65.4 1.7 copy.64
  67.1 0.3 pad_maximum_fusion
  67.3 0.2 slice_bitcast_fusion
  67.6 0.2 fusion.347
  67.9 0.2 fusion.345
  68.1 0.4 fusion.32
  68.5 1.2 copy.66
  69.8 0.5 broadcast_compare_fusion.27
  70.3 0.7 select_dynamic-update-slice_fusion.4
  71.1 0.7 select_dynamic-update-slice_fusion.3
  71.8 0.7 select_dynamic-update-slice_fusion.2
  72.5 0.7 select_dynamic-update-slice_fusion.1
  73.2 0.7 select_dynamic-update-slice_fusion
  73.9 0.1 select_add_fusion
  74.1 42.7 %all-gather.3.cloned.1.call-done = f32[220,1,2048]{2,1,0:T(1,128)} async-done(((f32[55,1,2048]{2,1,0:T(1,128)}), f32[220,1,2048]{2,1,0:T(1,128)}) %all-gather.3.cloned.1.call-update) | async-done | bytes 1802256 | tf_op jit(solution)/shard_map/all_gather | solution.py:142
  116.8 5.9 %multiply_reduce_fusion = f32[55,2048]{1,0:T(8,128)S(1)} fusion(f32[10,55,220]{2,1,0:T(8,128)} %select_dynamic-update-slice_fusion, f32[10,2048]{1,0:T(8,128)S(1)} %multiply_bitcast_fusion.1, f32[220,1,2048]{2,1,0:T(1,128)} %all-gather.3.cloned.1.call-done), kind=kOutput, calls=%fused_computation | convolution fusion | flops 2975836160 | bytes 2818720 | tf_op jit(solution)/shard_map/mij,jc->mic/dot_general | solution.py:139
  122.8 0.4 fusion.40
  123.2 0.2 slice_bitcast_fusion.2
  123.5 0.2 slice_bitcast_fusion.4
  123.7 3.1 %collective-permute-start.2 = (f32[55,1,2048]{2,0,1:T(8,128)S(1)}, f32[55,1,2048]{2,0,1:T(8,128)S(1)}, u32[]{:S(2)}, u32[]{:S(2)}) collective-permute-start(f32[55,1,2048]{2,0,1:T(8,128)S(1)} %fusion.40), channel_id=1, source_target_pairs={{4,0},{8,4},{12,8},{16,12},{20,16},{24,20},{28,24},{32,28},{36,32}... | collective-permute-start | bytes 1351688 | tf_op jit(solution)/shard_map/ppermute | solution.py:25
  126.8 6.6 %collective-permute-start.3 = (f32[55,1,2048]{2,0,1:T(8,128)S(1)}, f32[55,1,2048]{2,0,1:T(8,128)S(1)}, u32[]{:S(2)}, u32[]{:S(2)}) collective-permute-start(f32[55,1,2048]{2,0,1:T(8,128)S(1)} %fusion.40), channel_id=1, source_target_pairs={{0,4},{4,8},{8,12},{12,16},{16,20},{20,24},{24,28},{28,32},{32,36}... | collective-permute-start | bytes 1351688 | tf_op jit(solution)/shard_map/ppermute | solution.py:22
  133.3 0.2 fusion.36
  133.5 0.2 fusion.34
  133.7 9.7 %collective-permute-done.2 = f32[55,1,2048]{2,0,1:T(8,128)S(1)} collective-permute-done((f32[55,1,2048]{2,0,1:T(8,128)S(1)}, f32[55,1,2048]{2,0,1:T(8,128)S(1)}, u32[]{:S(2)}, u32[]{:S(2)}) %collective-permute-start.2) | collective-permute-done | bytes 450592 | tf_op jit(solution)/shard_map/ppermute | solution.py:25
  143.4 11.2 %collective-permute-done.3 = f32[55,1,2048]{2,0,1:T(8,128)S(1)} collective-permute-done((f32[55,1,2048]{2,0,1:T(8,128)S(1)}, f32[55,1,2048]{2,0,1:T(8,128)S(1)}, u32[]{:S(2)}, u32[]{:S(2)}) %collective-permute-start.3) | collective-permute-done | bytes 450592 | tf_op jit(solution)/shard_map/ppermute | solution.py:22
  154.8 3.1 %copy.71 = f32[3,55,1,2048]{1,0,2,3:T(4,128)} copy(f32[3,55,1,2048]{3,1,2,0:T(8,128)S(1)} %pad_maximum_fusion.1) | data formatting | bytes 2703360 | tf_op jit(solution)/shard_map/stack | solution.py:55
  157.9 6.6 %reshape.2106 = f32[4,1,84480]{2,1,0:T(1,128)} reshape(f32[2048,1,3,55]{3,2,1,0:T(4,128)} %bitcast.196) | data formatting | bytes 2703360
  164.6 3.7 %all-to-all-start = ((f32[4,1,84480]{2,1,0:T(1,128)}), f32[4,1,84480]{2,1,0:T(1,128)S(1)}, u32[]{:S(2)}, u32[]{:S(2)}) async-start(f32[4,1,84480]{2,1,0:T(1,128)} %reshape.2106), calls=%async_computation | async-start | bytes 2703360 | tf_op jit(solution)/shard_map/all_to_all | solution.py:157
  168.3 0.2 fusion.2
  168.6 1.1 fusion.343
  169.7 29.8 %all-to-all-done = f32[4,1,84480]{2,1,0:T(1,128)S(1)} async-done(((f32[4,1,84480]{2,1,0:T(1,128)}), f32[4,1,84480]{2,1,0:T(1,128)S(1)}, u32[]{:S(2)}, u32[]{:S(2)}) %all-to-all-start) | async-done | bytes 1351712 | tf_op jit(solution)/shard_map/all_to_all | solution.py:157
  199.6 0.5 broadcast.1558
  200.1 5.6 %reduce.20 = f32[4,84480]{1,0:T(4,128)} reduce(f32[4,1,84480]{2,1,0:T(1,128)S(1)} %all-to-all-done, f32[]{:T(128)} %broadcast.1558), dimensions={1}, to_apply=%all_to_all.24.reduce_sub_computation | reduce | bytes 2703364 | tf_op jit(solution)/shard_map/all_to_all | solution.py:157
  205.7 6.9 %reshape.2107 = f32[2048,1,3,55]{3,2,1,0:T(4,128)} reshape(f32[4,84480]{1,0:T(4,128)} %reduce.20) | data formatting | bytes 2703360
  212.6 4.6 %copy.79 = f32[3,55,1,4,512]{4,3,1,0,2:T(4,128)} copy(f32[3,55,1,4,512]{1,0,4,3,2:T(4,128)} %bitcast.197) | data formatting | bytes 2703360 | tf_op jit(solution)/shard_map/all_to_all | solution.py:157
  217.2 1.8 copy.73
  219.0 1.3 reshape.2092
  220.3 6.3 %multiply_reduce_fusion.1 = f32[512,512]{1,0:T(8,128)S(1)} fusion(f32[3,220,512]{2,1,0:T(8,128)} %reshape.2092, f32[512]{0:T(512)S(1)} %bitcast.231, f32[512]{0:T(512)S(1)} %bitcast.279, f32[512]{0:T(512)S(1)} %bitcast.259, f32[220]{0:T(256)S(1)} %get-tuple-element.133, f32[512]{0:T(512)S(1)} %bitcast.233, f32[512]{0:T(512)S(1)} %bitcast.277, ...), kind=kOutput, calls=%fused_computation.1 | convolution fusion | flops 2084474880 | bytes 2469412 | tf_op jit(solution)/shard_map/qi,kixn->kqxn/dot_general | solution.py:154
  226.6 3.1 %convolution_bitcast_fusion = f32[220,1,512]{2,0,1:T(8,128)S(1)} fusion(f32[512,512]{1,0:T(8,128)S(1)} %multiply_reduce_fusion.1, f32[512]{0:T(512)S(1)} %bitcast.285, f32[512]{0:T(512)S(1)} %bitcast.286, f32[512]{0:T(512)S(1)} %bitcast.287, f32[512]{0:T(512)S(1)} %bitcast.284, f32[512]{0:T(512)S(1)} %bitcast.283, pred[512]{0:T(512)(128)(4,1)S(1)} %copy-done.13, ...), kind=kOutput, calls=%fused_computation.8 | convolution fusion | flops 701628416 | bytes 1582628 | tf_op jit(solution)/shard_map/iq,qxn->ixn/dot_general | solution.py:176
  229.7 1.2 copy.74
  230.9 3.7 %all-to-all-start.1 = ((f32[220,1,512]{2,1,0:T(1,128)}), f32[220,1,512]{2,1,0:T(1,128)S(1)}, u32[]{:S(2)}, u32[]{:S(2)}) async-start(f32[220,1,512]{2,1,0:T(1,128)} %copy.74), calls=%async_computation.1 | async-start | bytes 901120 | tf_op jit(solution)/shard_map/all_to_all | solution.py:177
  234.7 0.2 fusion.341
  234.9 1.2 copy.77
  236.2 11.5 %all-to-all-done.1 = f32[220,1,512]{2,1,0:T(1,128)S(1)} async-done(((f32[220,1,512]{2,1,0:T(1,128)}), f32[220,1,512]{2,1,0:T(1,128)S(1)}, u32[]{:S(2)}, u32[]{:S(2)}) %all-to-all-start.1) | async-done | bytes 450592 | tf_op jit(solution)/shard_map/all_to_all | solution.py:177
  247.7 1.9 reduce.11
  249.6 1.9 all_to_all.28
  251.6 2.1 copy.75
  253.6 2.1 all_to_all.30
  255.7 1.7 fusion.28
  257.4 1.2 copy.78
  (69 shorter events, 1.3 us)
Async XLA Ops:
  7.2 109.7 %all-gather.3.cloned.1.call-start = ((), (), s32[]{:S(2)}) async-start(), calls=%async_computation.2 | async-start | bytes 2252800 | tf_op jit(solution)/shard_map/all_gather | solution.py:142
  8.7 14.0 %copy-start.4 = (s32[220,9]{0,1:T(8,128)S(1)}, s32[220,9]{0,1:T(8,128)}, u32[]{:S(2)}) copy-start(s32[220,9]{0,1:T(8,128)} %param.15) | copy-start | bytes 23764
  8.7 14.9 %copy-start.7 = (s32[1,2048]{1,0:T(1,128)S(1)}, s32[1,2048]{1,0:T(1,128)}, u32[]{:S(2)}) copy-start(s32[1,2048]{1,0:T(1,128)} %param.13) | copy-start | bytes 24580
  8.8 15.6 %copy-start.5 = (f32[1,2048]{1,0:T(1,128)S(1)}, f32[1,2048]{1,0:T(1,128)}, u32[]{:S(2)}) copy-start(f32[1,2048]{1,0:T(1,128)} %param.12) | copy-start | bytes 24580
  8.8 15.6 %copy-start.8 = (s32[512]{0:T(512)S(1)}, s32[512]{0:T(512)}, u32[]{:S(2)}) copy-start(s32[512]{0:T(512)} %param.17) | copy-start | bytes 6148
  8.8 16.4 %copy-start.9 = (f32[4,9]{1,0:T(4,128)S(1)}, f32[4,9]{1,0:T(4,128)}, u32[]{:S(2)}) copy-start(f32[4,9]{1,0:T(4,128)} %param.14) | copy-start | bytes 436
  9.5 45.6 %collective-permute-start.1 = (f32[2,55,1,2048]{3,0,2,1:T(2,128)S(1)}, f32[2,55,1,2048]{3,0,2,1:T(2,128)}, u32[]{:S(2)}, u32[]{:S(2)}) collective-permute-start(f32[2,55,1,2048]{3,0,2,1:T(2,128)S(1)} %copy.62), channel_id=1, source_target_pairs={{4,0},{8,4},{12,8},{16,12},{20,16},{24,20},{28,24},{32,28},{36,32}... | collective-permute-start | bytes 2703368 | tf_op jit(solution)/shard_map/ppermute | solution.py:25
  12.1 53.3 %collective-permute-start = (f32[2,55,1,2048]{3,0,2,1:T(2,128)S(1)}, f32[2,55,1,2048]{3,0,2,1:T(2,128)}, u32[]{:S(2)}, u32[]{:S(2)}) collective-permute-start(f32[2,55,1,2048]{3,0,2,1:T(2,128)S(1)} %copy.62), channel_id=1, source_target_pairs={{0,4},{4,8},{8,12},{12,16},{16,20},{20,24},{24,28},{28,32},{32,36}... | collective-permute-start | bytes 2703368 | tf_op jit(solution)/shard_map/ppermute | solution.py:22
  74.1 48.7 %copy-start.2 = (f32[55,1,2048]{2,1,0:T(1,128)S(1)}, f32[55,1,2048]{2,1,0:T(1,128)}, u32[]{:S(2)}) copy-start(f32[55,1,2048]{2,1,0:T(1,128)} %param.9) | copy-start | bytes 1351684
  74.1 48.7 %copy-start.3 = (f32[55,1,2048]{2,1,0:T(1,128)S(1)}, f32[55,1,2048]{2,1,0:T(1,128)}, u32[]{:S(2)}) copy-start(f32[55,1,2048]{2,1,0:T(1,128)} %param.10) | copy-start | bytes 1351684
  123.7 19.7 %collective-permute-start.2 = (f32[55,1,2048]{2,0,1:T(8,128)S(1)}, f32[55,1,2048]{2,0,1:T(8,128)S(1)}, u32[]{:S(2)}, u32[]{:S(2)}) collective-permute-start(f32[55,1,2048]{2,0,1:T(8,128)S(1)} %fusion.40), channel_id=1, source_target_pairs={{4,0},{8,4},{12,8},{16,12},{20,16},{24,20},{28,24},{32,28},{36,32}... | collective-permute-start | bytes 1351688 | tf_op jit(solution)/shard_map/ppermute | solution.py:25
  126.8 27.9 %collective-permute-start.3 = (f32[55,1,2048]{2,0,1:T(8,128)S(1)}, f32[55,1,2048]{2,0,1:T(8,128)S(1)}, u32[]{:S(2)}, u32[]{:S(2)}) collective-permute-start(f32[55,1,2048]{2,0,1:T(8,128)S(1)} %fusion.40), channel_id=1, source_target_pairs={{0,4},{4,8},{8,12},{12,16},{16,20},{20,24},{24,28},{28,32},{32,36}... | collective-permute-start | bytes 1351688 | tf_op jit(solution)/shard_map/ppermute | solution.py:22
  164.6 3.7 %copy-start.6 = (s32[512,9]{0,1:T(8,128)S(1)}, s32[512,9]{0,1:T(8,128)}, u32[]{:S(2)}) copy-start(s32[512,9]{0,1:T(8,128)} %param.16) | copy-start | bytes 55300
  164.6 35.0 %all-to-all-start = ((f32[4,1,84480]{2,1,0:T(1,128)}), f32[4,1,84480]{2,1,0:T(1,128)S(1)}, u32[]{:S(2)}, u32[]{:S(2)}) async-start(f32[4,1,84480]{2,1,0:T(1,128)} %reshape.2106), calls=%async_computation | async-start | bytes 2703360 | tf_op jit(solution)/shard_map/all_to_all | solution.py:157
  220.2 6.3 %copy-start.10 = (pred[512]{0:T(512)(128)(4,1)S(1)}, pred[512]{0:T(512)(128)(4,1)}, u32[]{:S(2)}) copy-start(pred[512]{0:T(512)(128)(4,1)} %get-tuple-element.12) | copy-start | bytes 1540
  220.2 6.3 %copy-start.11 = (pred[512]{0:T(512)(128)(4,1)S(1)}, pred[512]{0:T(512)(128)(4,1)}, u32[]{:S(2)}) copy-start(pred[512]{0:T(512)(128)(4,1)} %get-tuple-element.13) | copy-start | bytes 1540
  220.3 6.3 %copy-start.12 = (pred[512]{0:T(512)(128)(4,1)S(1)}, pred[512]{0:T(512)(128)(4,1)}, u32[]{:S(2)}) copy-start(pred[512]{0:T(512)(128)(4,1)} %get-tuple-element.14) | copy-start | bytes 1540
  220.3 6.3 %copy-start.13 = (pred[512]{0:T(512)(128)(4,1)S(1)}, pred[512]{0:T(512)(128)(4,1)}, u32[]{:S(2)}) copy-start(pred[512]{0:T(512)(128)(4,1)} %get-tuple-element.15) | copy-start | bytes 1540
  220.3 6.3 %copy-start.14 = (pred[220]{0:T(512)(128)(4,1)S(1)}, pred[220]{0:T(512)(128)(4,1)}, u32[]{:S(2)}) copy-start(pred[220]{0:T(512)(128)(4,1)} %get-tuple-element.106) | copy-start | bytes 664
  220.3 6.3 %copy-start.15 = (pred[220]{0:T(512)(128)(4,1)S(1)}, pred[220]{0:T(512)(128)(4,1)}, u32[]{:S(2)}) copy-start(pred[220]{0:T(512)(128)(4,1)} %get-tuple-element.107) | copy-start | bytes 664
  220.3 6.3 %copy-start.16 = (pred[220]{0:T(512)(128)(4,1)S(1)}, pred[220]{0:T(512)(128)(4,1)}, u32[]{:S(2)}) copy-start(pred[220]{0:T(512)(128)(4,1)} %get-tuple-element.108) | copy-start | bytes 664
  230.9 16.8 %all-to-all-start.1 = ((f32[220,1,512]{2,1,0:T(1,128)}), f32[220,1,512]{2,1,0:T(1,128)S(1)}, u32[]{:S(2)}, u32[]{:S(2)}) async-start(f32[220,1,512]{2,1,0:T(1,128)} %copy.74), calls=%async_computation.1 | async-start | bytes 901120 | tf_op jit(solution)/shard_map/all_to_all | solution.py:177
  249.6 6.1 %copy-start = (f32[55,1,2047]{2,0,1:T(8,128)S(1)}, f32[55,1,2047]{2,0,1:T(8,128)}, u32[]{:S(2)}) copy-start(f32[55,1,2047]{2,0,1:T(8,128)} %get-tuple-element.30) | copy-start | bytes 1351024
  249.6 6.1 %copy-start.1 = (f32[55,1,2047]{2,0,1:T(8,128)S(1)}, f32[55,1,2047]{2,0,1:T(8,128)}, u32[]{:S(2)}) copy-start(f32[55,1,2047]{2,0,1:T(8,128)} %get-tuple-element.31) | copy-start | bytes 1351024
Sparse Core Ops, SparseCore 0:
  69.9 46.8 all-gather.2
where the time goes:
time: 266 us
  waiting for transfers between devices  141 us (53%)
  local copies, waits for them, and re-layouts  44.4 us (17%)
  starting transfers between devices  30.2 us (11%)
  other arithmetic  19.7 us (7%)
  matrix products  15.4 us (6%)
  between operations  14.5 us (5%)
    all_gather x1, waiting for transfers between devices, on_device(): lax.all_gather(flat_rough, 'modes', axis=0, tiled=True)  42.7 us
    ppermute x2, waiting for transfers between devices, padded_2(): lax.ppermute(lax.slice_in_dim(block, 0, width, axis=dim), axis, backward)  37.3 us
    all_to_all x1, waiting for transfers between devices, on_device(): lax.all_to_all(grads, 'modes', split_axis=3, concat_axis=1, tiled=True)  29.8 us
    ppermute x2, waiting for transfers between devices, padded_2(): lax.ppermute(lax.slice_in_dim(block, block.shape[dim] - width, None, axis...  19.9 us
    unnamed x39, local copies, waits for them, and re-layouts  17.5 us
    ppermute x2, starting transfers between devices, padded_2(): lax.ppermute(lax.slice_in_dim(block, block.shape[dim] - width, None, axis...  17.1 us
    all_to_all x1, waiting for transfers between devices, on_device(): lax.all_to_all(heat_points, 'modes', split_axis=0, concat_axis=2, tiled=T...  11.5 us
    all_to_all x3, local copies, waits for them, and re-layouts, on_device(): lax.all_to_all(grads, 'modes', split_axis=3, concat_axis=1, tiled=True)  6.9 us
  transfers between devices with their start and end apart: 7, of which 7 were waited for; matrix products, arithmetic and copies ran while one was open for 5% of the time, Pallas kernels for 0%

commit v1 on v0

--- a/solution.py
+++ b/solution.py
@@ -12,6 +12,19 @@
     2.8569700138728056,
     -2.8569700138728056,
 )
+
+
+def wait_rates_in(array_here, on_dim):
+    arr_next = jnp.concatenate(
+        lax.all_to_all(
+            jnp.stack([array_here] * lax.axis_size("modes")),
+            axis_name="modes",
+            split_axis=0,
+            concat_axis=0,
+        ),
+        on_dim,
+    )
+    return arr_next
 
 
 def padded_2(block, sides, width):
@@ -136,12 +149,7 @@
     coeff_flat = coeff.reshape(coeff.shape[0], cell_count)
     flat_rough = diffusion_operator_weights(pot_padded).reshape(modes_here, cell_count)
     row_coup = coupling(own_table, polynomial_exponent_rows)
-    mixed = jnp.einsum(
-        "mij,jc->mic",
-        row_coup,
-        lax.all_gather(flat_rough, "modes", axis=0, tiled=True),
-        precision=hp,
-    )
+    mixed = jnp.einsum("mij,jc->mic", row_coup, wait_rates_in(flat_rough, on_dim=0), precision=hp)
     applied = jnp.sum(coeff_flat[:, None, :] * mixed, axis=0)
     applied = applied.reshape(modes_here, planes, columns)
     relaxed_voltage = voltage_expansion + 0.8 * (current_injection - applied) / (

time: 266 us -> 238 us (0.89)
  the two profiles are of different devices: /device:TPU:59 before, /device:TPU:5 now
where the time goes in v1:
time: 238 us; the launch traced here: 237 us
  waiting for transfers between devices  120 us (50%)
  local copies, waits for them, and re-layouts  46.3 us (19%)
  starting transfers between devices  35.5 us (15%)
  other arithmetic  19.7 us (8%)
  matrix products  14.8 us (6%)
    ppermute x2, waiting for transfers between devices, padded_2(): lax.ppermute(lax.slice_in_dim(block, 0, width, axis=dim), axis, backward)  41.5 us
    all_to_all x1, waiting for transfers between devices, wait_rates_in(): lax.all_to_all(jnp.stack([array_here] * lax.axis_size('modes')), axis_nam...  31.3 us
    all_to_all x1, waiting for transfers between devices, on_device(): lax.all_to_all(grads, 'modes', split_axis=3, concat_axis=1, tiled=True)  28.5 us
    ppermute x2, starting transfers between devices, padded_2(): lax.ppermute(lax.slice_in_dim(block, block.shape[dim] - width, None, axis...  18.1 us
    unnamed x39, local copies, waits for them, and re-layouts  17.5 us
    all_to_all x1, waiting for transfers between devices, on_device(): lax.all_to_all(heat_points, 'modes', split_axis=0, concat_axis=2, tiled=T...  11.5 us
    ppermute x2, waiting for transfers between devices, padded_2(): lax.ppermute(lax.slice_in_dim(block, block.shape[dim] - width, None, axis...  7.18 us
    all_to_all x3, local copies, waits for them, and re-layouts, on_device(): lax.all_to_all(grads, 'modes', split_axis=3, concat_axis=1, tiled=True)  6.9 us
  transfers between devices with their start and end apart: 7, of which 6 were waited for; matrix products, arithmetic and copies ran while one was open for 6% of the time, Pallas kernels for 0%

profile of v1, /device:TPU:5, one launch (start us, length us, event | category | flops | bytes accessed | tf_op | source)
XLA Modules:
  0.0 237.4 jit_solution(10916193212295268948)
XLA Ops:
  0.6 1.4 copy_bitcast_fusion
  2.2 0.7 copy.67
  2.9 2.6 %collective-permute-start.1 = (f32[2,55,1,2048]{3,0,2,1:T(2,128)S(1)}, f32[2,55,1,2048]{3,0,2,1:T(2,128)}, u32[]{:S(2)}, u32[]{:S(2)}) collective-permute-start(f32[2,55,1,2048]{3,0,2,1:T(2,128)S(1)} %copy.67), channel_id=1, source_target_pairs={{4,0},{8,4},{12,8},{16,12},{20,16},{24,20},{28,24},{32,28},{36,32}... | collective-permute-start | bytes 2703368 | tf_op jit(solution)/shard_map/ppermute | solution.py:38
  5.5 10.5 %collective-permute-start = (f32[2,55,1,2048]{3,0,2,1:T(2,128)S(1)}, f32[2,55,1,2048]{3,0,2,1:T(2,128)}, u32[]{:S(2)}, u32[]{:S(2)}) collective-permute-start(f32[2,55,1,2048]{3,0,2,1:T(2,128)S(1)} %copy.67), channel_id=1, source_target_pairs={{0,4},{4,8},{8,12},{12,16},{16,20},{20,24},{24,28},{28,32},{32,36}... | collective-permute-start | bytes 2703368 | tf_op jit(solution)/shard_map/ppermute | solution.py:35
  16.3 0.1 broadcast_subtract_fusion
  16.5 0.6 bitcast_dynamic-update-slice_fusion
  17.2 0.6 compare_reduce_fusion.7
  17.9 0.7 select_dynamic-update-slice_fusion.8
  18.7 0.7 select_dynamic-update-slice_fusion.7
  19.4 0.7 select_dynamic-update-slice_fusion.6
  20.1 0.7 select_dynamic-update-slice_fusion.5
  20.8 26.7 %collective-permute-done.1 = f32[2,55,1,2048]{3,0,2,1:T(2,128)} collective-permute-done((f32[2,55,1,2048]{3,0,2,1:T(2,128)S(1)}, f32[2,55,1,2048]{3,0,2,1:T(2,128)}, u32[]{:S(2)}, u32[]{:S(2)}) %collective-permute-start.1) | collective-permute-done | bytes 901152 | tf_op jit(solution)/shard_map/ppermute | solution.py:38
  47.5 1.7 copy.70
  49.2 7.2 %collective-permute-done = f32[2,55,1,2048]{3,0,2,1:T(2,128)} collective-permute-done((f32[2,55,1,2048]{3,0,2,1:T(2,128)S(1)}, f32[2,55,1,2048]{3,0,2,1:T(2,128)}, u32[]{:S(2)}, u32[]{:S(2)}) %collective-permute-start) | collective-permute-done | bytes 901152 | tf_op jit(solution)/shard_map/ppermute | solution.py:35
  56.4 1.7 copy.69
  58.1 0.3 pad_maximum_fusion
  58.4 0.2 slice_bitcast_fusion
  58.7 0.2 fusion.346
  59.0 0.2 fusion.344
  59.2 0.4 fusion.31
  59.6 1.4 stack.18
  61.0 4.4 %all-to-all-start = ((f32[4,55,2048]{2,1,0:T(8,128)}), f32[4,55,2048]{2,1,0:T(8,128)}, u32[]{:S(2)}, u32[]{:S(2)}) async-start(f32[4,55,2048]{2,1,0:T(8,128)} %stack.18), calls=%async_computation | async-start | bytes 3670016 | tf_op jit(solution)/shard_map/all_to_all | solution.py:19
  65.4 0.6 broadcast_compare_fusion.27
  66.0 0.7 select_dynamic-update-slice_fusion.4
  66.7 0.7 select_dynamic-update-slice_fusion.3
  67.4 0.7 select_dynamic-update-slice_fusion.2
  68.1 0.7 select_dynamic-update-slice_fusion.1
  68.8 0.7 select_dynamic-update-slice_fusion
  69.7 31.3 %all-to-all-done = f32[4,55,2048]{2,1,0:T(8,128)} async-done(((f32[4,55,2048]{2,1,0:T(8,128)}), f32[4,55,2048]{2,1,0:T(8,128)}, u32[]{:S(2)}, u32[]{:S(2)}) %all-to-all-start) | async-done | bytes 1802272 | tf_op jit(solution)/shard_map/all_to_all | solution.py:19
  101.0 1.7 reshape.2095
  102.7 5.3 %multiply_reduce_fusion = f32[55,2048]{1,0:T(8,128)S(1)} fusion(f32[10,55,220]{2,1,0:T(8,128)} %select_dynamic-update-slice_fusion, f32[220,2048,1]{1,0,2:T(8,128)S(1)} %reshape.2095, f32[10,2048]{1,0:T(8,128)S(1)} %multiply_bitcast_fusion.1), kind=kOutput, calls=%fused_computation | convolution fusion | flops 2975836160 | bytes 2818720 | tf_op jit(solution)/shard_map/mij,jc->mic/dot_general | solution.py:152
  108.0 0.4 fusion.39
  108.5 0.2 slice_bitcast_fusion.2
  108.7 0.2 slice_bitcast_fusion.4
  108.9 1.9 collective-permute-start.2
  110.9 7.5 %collective-permute-start.3 = (f32[55,1,2048]{2,0,1:T(8,128)S(1)}, f32[55,1,2048]{2,0,1:T(8,128)S(1)}, u32[]{:S(2)}, u32[]{:S(2)}) collective-permute-start(f32[55,1,2048]{2,0,1:T(8,128)S(1)} %fusion.39), channel_id=1, source_target_pairs={{0,4},{4,8},{8,12},{12,16},{16,20},{20,24},{24,28},{28,32},{32,36}... | collective-permute-start | bytes 1351688 | tf_op jit(solution)/shard_map/ppermute | solution.py:35
  118.4 0.2 fusion.35
  118.6 0.2 fusion.33
  118.8 14.8 %collective-permute-done.2 = f32[55,1,2048]{2,0,1:T(8,128)S(1)} collective-permute-done((f32[55,1,2048]{2,0,1:T(8,128)S(1)}, f32[55,1,2048]{2,0,1:T(8,128)S(1)}, u32[]{:S(2)}, u32[]{:S(2)}) %collective-permute-start.2) | collective-permute-done | bytes 450592 | tf_op jit(solution)/shard_map/ppermute | solution.py:38
  133.8 3.1 %copy.75 = f32[3,55,1,2048]{1,0,2,3:T(4,128)} copy(f32[3,55,1,2048]{3,1,2,0:T(8,128)S(1)} %pad_maximum_fusion.1) | data formatting | bytes 2703360 | tf_op jit(solution)/shard_map/stack | solution.py:68
  136.9 6.6 %reshape.2107 = f32[4,1,84480]{2,1,0:T(1,128)} reshape(f32[2048,1,3,55]{3,2,1,0:T(4,128)} %bitcast.196) | data formatting | bytes 2703360
  143.5 4.8 %all-to-all-start.1 = ((f32[4,1,84480]{2,1,0:T(1,128)}), f32[4,1,84480]{2,1,0:T(1,128)S(1)}, u32[]{:S(2)}, u32[]{:S(2)}) async-start(f32[4,1,84480]{2,1,0:T(1,128)} %reshape.2107), calls=%async_computation.1 | async-start | bytes 2703360 | tf_op jit(solution)/shard_map/all_to_all | solution.py:165
  148.3 0.2 fusion
  148.7 1.1 fusion.342
  149.7 28.5 %all-to-all-done.1 = f32[4,1,84480]{2,1,0:T(1,128)S(1)} async-done(((f32[4,1,84480]{2,1,0:T(1,128)}), f32[4,1,84480]{2,1,0:T(1,128)S(1)}, u32[]{:S(2)}, u32[]{:S(2)}) %all-to-all-start.1) | async-done | bytes 1351712 | tf_op jit(solution)/shard_map/all_to_all | solution.py:165
  178.3 0.5 broadcast.1559
  178.8 5.7 %reduce.20 = f32[4,84480]{1,0:T(4,128)} reduce(f32[4,1,84480]{2,1,0:T(1,128)S(1)} %all-to-all-done.1, f32[]{:T(128)} %broadcast.1559), dimensions={1}, to_apply=%all_to_all.28.reduce_sub_computation | reduce | bytes 2703364 | tf_op jit(solution)/shard_map/all_to_all | solution.py:165
  184.4 6.9 %reshape.2108 = f32[2048,1,3,55]{3,2,1,0:T(4,128)} reshape(f32[4,84480]{1,0:T(4,128)} %reduce.20) | data formatting | bytes 2703360
  191.3 4.6 %copy.83 = f32[3,55,1,4,512]{4,3,1,0,2:T(4,128)} copy(f32[3,55,1,4,512]{1,0,4,3,2:T(4,128)} %bitcast.197) | data formatting | bytes 2703360 | tf_op jit(solution)/shard_map/all_to_all | solution.py:165
  196.0 1.8 copy.77
  197.7 1.3 reshape.2094
  199.0 6.3 %multiply_reduce_fusion.1 = f32[512,512]{1,0:T(8,128)S(1)} fusion(f32[3,220,512]{2,1,0:T(8,128)} %reshape.2094, f32[512]{0:T(512)S(1)} %bitcast.231, f32[512]{0:T(512)S(1)} %bitcast.279, f32[512]{0:T(512)S(1)} %bitcast.259, f32[220]{0:T(256)S(1)} %get-tuple-element.133, f32[512]{0:T(512)S(1)} %bitcast.233, f32[512]{0:T(512)S(1)} %bitcast.277, ...), kind=kOutput, calls=%fused_computation.1 | convolution fusion | flops 2084474880 | bytes 2469412 | tf_op jit(solution)/shard_map/qi,kixn->kqxn/dot_general | solution.py:162
  205.4 3.1 %convolution_bitcast_fusion = f32[220,1,512]{2,0,1:T(8,128)S(1)} fusion(f32[512,512]{1,0:T(8,128)S(1)} %multiply_reduce_fusion.1, f32[512]{0:T(512)S(1)} %bitcast.285, f32[512]{0:T(512)S(1)} %bitcast.286, f32[512]{0:T(512)S(1)} %bitcast.287, f32[512]{0:T(512)S(1)} %bitcast.284, f32[512]{0:T(512)S(1)} %bitcast.283, pred[512]{0:T(512)(128)(4,1)S(1)} %copy-done.13, ...), kind=kOutput, calls=%fused_computation.6 | convolution fusion | flops 701628416 | bytes 1582628 | tf_op jit(solution)/shard_map/iq,qxn->ixn/dot_general | solution.py:184
  208.4 1.2 copy.78
  209.7 3.7 %all-to-all-start.2 = ((f32[220,1,512]{2,1,0:T(1,128)}), f32[220,1,512]{2,1,0:T(1,128)S(1)}, u32[]{:S(2)}, u32[]{:S(2)}) async-start(f32[220,1,512]{2,1,0:T(1,128)} %copy.78), calls=%async_computation.2 | async-start | bytes 901120 | tf_op jit(solution)/shard_map/all_to_all | solution.py:185
  213.5 0.2 fusion.340
  213.7 1.2 copy.81
  214.9 11.5 %all-to-all-done.2 = f32[220,1,512]{2,1,0:T(1,128)S(1)} async-done(((f32[220,1,512]{2,1,0:T(1,128)}), f32[220,1,512]{2,1,0:T(1,128)S(1)}, u32[]{:S(2)}, u32[]{:S(2)}) %all-to-all-start.2) | async-done | bytes 450592 | tf_op jit(solution)/shard_map/all_to_all | solution.py:185
  226.4 1.9 reduce.11
  228.3 1.9 all_to_all.32
  230.3 2.1 copy.79
  232.4 2.1 all_to_all.34
  234.5 1.7 fusion.26
  236.2 1.2 copy.82
  (69 shorter events, 1.4 us)
Async XLA Ops:
  2.1 14.0 %copy-start.4 = (s32[220,9]{0,1:T(8,128)S(1)}, s32[220,9]{0,1:T(8,128)}, u32[]{:S(2)}) copy-start(s32[220,9]{0,1:T(8,128)} %param.15) | copy-start | bytes 23764
  2.2 14.9 %copy-start.7 = (s32[1,2048]{1,0:T(1,128)S(1)}, s32[1,2048]{1,0:T(1,128)}, u32[]{:S(2)}) copy-start(s32[1,2048]{1,0:T(1,128)} %param.13) | copy-start | bytes 24580
  2.2 15.7 %copy-start.5 = (f32[1,2048]{1,0:T(1,128)S(1)}, f32[1,2048]{1,0:T(1,128)}, u32[]{:S(2)}) copy-start(f32[1,2048]{1,0:T(1,128)} %param.12) | copy-start | bytes 24580
  2.2 15.6 %copy-start.8 = (s32[512]{0:T(512)S(1)}, s32[512]{0:T(512)}, u32[]{:S(2)}) copy-start(s32[512]{0:T(512)} %param.17) | copy-start | bytes 6148
  2.2 16.5 %copy-start.9 = (f32[4,9]{1,0:T(4,128)S(1)}, f32[4,9]{1,0:T(4,128)}, u32[]{:S(2)}) copy-start(f32[4,9]{1,0:T(4,128)} %param.14) | copy-start | bytes 436
  2.9 44.6 %collective-permute-start.1 = (f32[2,55,1,2048]{3,0,2,1:T(2,128)S(1)}, f32[2,55,1,2048]{3,0,2,1:T(2,128)}, u32[]{:S(2)}, u32[]{:S(2)}) collective-permute-start(f32[2,55,1,2048]{3,0,2,1:T(2,128)S(1)} %copy.67), channel_id=1, source_target_pairs={{4,0},{8,4},{12,8},{16,12},{20,16},{24,20},{28,24},{32,28},{36,32}... | collective-permute-start | bytes 2703368 | tf_op jit(solution)/shard_map/ppermute | solution.py:38
  5.5 50.9 %collective-permute-start = (f32[2,55,1,2048]{3,0,2,1:T(2,128)S(1)}, f32[2,55,1,2048]{3,0,2,1:T(2,128)}, u32[]{:S(2)}, u32[]{:S(2)}) collective-permute-start(f32[2,55,1,2048]{3,0,2,1:T(2,128)S(1)} %copy.67), channel_id=1, source_target_pairs={{0,4},{4,8},{8,12},{12,16},{16,20},{20,24},{24,28},{28,32},{32,36}... | collective-permute-start | bytes 2703368 | tf_op jit(solution)/shard_map/ppermute | solution.py:35
  61.0 39.9 %all-to-all-start = ((f32[4,55,2048]{2,1,0:T(8,128)}), f32[4,55,2048]{2,1,0:T(8,128)}, u32[]{:S(2)}, u32[]{:S(2)}) async-start(f32[4,55,2048]{2,1,0:T(8,128)} %stack.18), calls=%async_computation | async-start | bytes 3670016 | tf_op jit(solution)/shard_map/all_to_all | solution.py:19
  102.7 5.3 %copy-start.2 = (f32[55,1,2048]{2,1,0:T(1,128)S(1)}, f32[55,1,2048]{2,1,0:T(1,128)}, u32[]{:S(2)}) copy-start(f32[55,1,2048]{2,1,0:T(1,128)} %param.9) | copy-start | bytes 1351684
  102.7 5.3 %copy-start.3 = (f32[55,1,2048]{2,1,0:T(1,128)S(1)}, f32[55,1,2048]{2,1,0:T(1,128)}, u32[]{:S(2)}) copy-start(f32[55,1,2048]{2,1,0:T(1,128)} %param.10) | copy-start | bytes 1351684
  108.9 24.7 %collective-permute-start.2 = (f32[55,1,2048]{2,0,1:T(8,128)S(1)}, f32[55,1,2048]{2,0,1:T(8,128)S(1)}, u32[]{:S(2)}, u32[]{:S(2)}) collective-permute-start(f32[55,1,2048]{2,0,1:T(8,128)S(1)} %fusion.39), channel_id=1, source_target_pairs={{4,0},{8,4},{12,8},{16,12},{20,16},{24,20},{28,24},{32,28},{36,32}... | collective-permute-start | bytes 1351688 | tf_op jit(solution)/shard_map/ppermute | solution.py:38
  110.9 22.8 %collective-permute-start.3 = (f32[55,1,2048]{2,0,1:T(8,128)S(1)}, f32[55,1,2048]{2,0,1:T(8,128)S(1)}, u32[]{:S(2)}, u32[]{:S(2)}) collective-permute-start(f32[55,1,2048]{2,0,1:T(8,128)S(1)} %fusion.39), channel_id=1, source_target_pairs={{0,4},{4,8},{8,12},{12,16},{16,20},{20,24},{24,28},{28,32},{32,36}... | collective-permute-start | bytes 1351688 | tf_op jit(solution)/shard_map/ppermute | solution.py:35
  143.5 4.8 %copy-start.6 = (s32[512,9]{0,1:T(8,128)S(1)}, s32[512,9]{0,1:T(8,128)}, u32[]{:S(2)}) copy-start(s32[512,9]{0,1:T(8,128)} %param.16) | copy-start | bytes 55300
  143.5 34.7 %all-to-all-start.1 = ((f32[4,1,84480]{2,1,0:T(1,128)}), f32[4,1,84480]{2,1,0:T(1,128)S(1)}, u32[]{:S(2)}, u32[]{:S(2)}) async-start(f32[4,1,84480]{2,1,0:T(1,128)} %reshape.2107), calls=%async_computation.1 | async-start | bytes 2703360 | tf_op jit(solution)/shard_map/all_to_all | solution.py:165
  199.0 6.3 %copy-start.10 = (pred[512]{0:T(512)(128)(4,1)S(1)}, pred[512]{0:T(512)(128)(4,1)}, u32[]{:S(2)}) copy-start(pred[512]{0:T(512)(128)(4,1)} %get-tuple-element.12) | copy-start | bytes 1540
  199.0 6.3 %copy-start.11 = (pred[512]{0:T(512)(128)(4,1)S(1)}, pred[512]{0:T(512)(128)(4,1)}, u32[]{:S(2)}) copy-start(pred[512]{0:T(512)(128)(4,1)} %get-tuple-element.13) | copy-start | bytes 1540
  199.0 6.3 %copy-start.12 = (pred[512]{0:T(512)(128)(4,1)S(1)}, pred[512]{0:T(512)(128)(4,1)}, u32[]{:S(2)}) copy-start(pred[512]{0:T(512)(128)(4,1)} %get-tuple-element.14) | copy-start | bytes 1540
  199.0 6.3 %copy-start.13 = (pred[512]{0:T(512)(128)(4,1)S(1)}, pred[512]{0:T(512)(128)(4,1)}, u32[]{:S(2)}) copy-start(pred[512]{0:T(512)(128)(4,1)} %get-tuple-element.15) | copy-start | bytes 1540
  199.0 6.3 %copy-start.14 = (pred[220]{0:T(512)(128)(4,1)S(1)}, pred[220]{0:T(512)(128)(4,1)}, u32[]{:S(2)}) copy-start(pred[220]{0:T(512)(128)(4,1)} %get-tuple-element.106) | copy-start | bytes 664
  199.0 6.3 %copy-start.15 = (pred[220]{0:T(512)(128)(4,1)S(1)}, pred[220]{0:T(512)(128)(4,1)}, u32[]{:S(2)}) copy-start(pred[220]{0:T(512)(128)(4,1)} %get-tuple-element.107) | copy-start | bytes 664
  199.0 6.3 %copy-start.16 = (pred[220]{0:T(512)(128)(4,1)S(1)}, pred[220]{0:T(512)(128)(4,1)}, u32[]{:S(2)}) copy-start(pred[220]{0:T(512)(128)(4,1)} %get-tuple-element.108) | copy-start | bytes 664
  209.7 16.8 %all-to-all-start.2 = ((f32[220,1,512]{2,1,0:T(1,128)}), f32[220,1,512]{2,1,0:T(1,128)S(1)}, u32[]{:S(2)}, u32[]{:S(2)}) async-start(f32[220,1,512]{2,1,0:T(1,128)} %copy.78), calls=%async_computation.2 | async-start | bytes 901120 | tf_op jit(solution)/shard_map/all_to_all | solution.py:185
  228.3 6.1 %copy-start = (f32[55,1,2047]{2,0,1:T(8,128)S(1)}, f32[55,1,2047]{2,0,1:T(8,128)}, u32[]{:S(2)}) copy-start(f32[55,1,2047]{2,0,1:T(8,128)} %get-tuple-element.30) | copy-start | bytes 1351024
  228.3 6.1 %copy-start.1 = (f32[55,1,2047]{2,0,1:T(8,128)S(1)}, f32[55,1,2047]{2,0,1:T(8,128)}, u32[]{:S(2)}) copy-start(f32[55,1,2047]{2,0,1:T(8,128)} %get-tuple-element.31) | copy-start | bytes 1351024
